TPU v7x, 32 devices: a whole 2x2x4 slice. The times are simulated.
32 devices in a mesh: seq: 4 (over x, core), shard: 8 (over z, y).
Axes of the slice: x: 2, y: 2, z: 4, core: 2. Of those that a mesh axis runs over, the one named last changes fastest.
Arguments:
- inputs: bfloat16 [8, 3072, 768], P('shard', 'seq'), may hold values from -6 to 6
- teacher: bfloat16 [8, 3072, 768], P('shard', 'seq'), may hold values from -6 to 6
- seq_lengths: int32 [8, 3], P('shard'), may hold values from 0 to 3072, as said below
- w_qkv: bfloat16 [768, 2304], P('shard'), may hold values from -0.21875 to 0.21875
- q_bias: bfloat16 [768], P('shard'), may hold values from -4 to 4
- v_bias: bfloat16 [768], P('shard'), may hold values from -0.75 to 0.75
- w_out: bfloat16 [768, 768], P('shard'), may hold values from -3.5 to 3.5
- out_bias: bfloat16 [768], P('shard'), may hold values from -4 to 4
- attn_gain: bfloat16 [768], P('shard'), may hold values from 0.5 to 1.5
- attn_shift: bfloat16 [768], P('shard'), may hold values from -4 to 4
- w_up: bfloat16 [768, 3072], P('shard'), may hold values from -0.21875 to 0.21875
- up_bias: bfloat16 [3072], P('shard'), may hold values from -4 to 4
- w_down: bfloat16 [3072, 768], P('shard'), may hold values from -0.109375 to 0.109375
- down_bias: bfloat16 [768], P('shard'), may hold values from -4 to 4
- ffn_gain: bfloat16 [768], P('shard'), may hold values from 0.5 to 1.5
- ffn_shift: bfloat16 [768], P('shard'), may hold values from -4 to 4
Outputs:
- layer_out: bfloat16 [8, 3072, 768], P('shard', 'seq')
- input_grad: bfloat16 [8, 3072, 768], P('shard', 'seq')
- grad_qkv: float32 [768, 2304], P('shard')
- grad_q_bias: float32 [768], P('shard')
- grad_v_bias: float32 [768], P('shard')
- grad_out: float32 [768, 768], P('shard')
- grad_out_bias: float32 [768], P('shard')
- grad_attn_gain: float32 [768], P('shard')
- grad_attn_shift: float32 [768], P('shard')
- grad_up: float32 [768, 3072], P('shard')
- grad_up_bias: float32 [3072], P('shard')
- grad_down: float32 [3072, 768], P('shard')
- grad_down_bias: float32 [768], P('shard')
- grad_ffn_gain: float32 [768], P('shard')
- grad_ffn_shift: float32 [768], P('shard')
Inputs may be any that keep to these rules, and one draw needn't show every extreme that they name: `seq_lengths`: each row lists the lengths of the sequences packed from the start of one group's 3072 slots; the used slots come first and each holds 1024 tokens or more, the unused ones are 0; a row sums to at most 3072; some row holds a single sequence of 3072 tokens; the slots after a row's sum are padding.
All inputs are finite; a program needn't handle non-finite values.
Results may differ from a plain program's by a relative error of at most 0.01.
Values may be sent and summed in bfloat16 or wider, within the bound.
A program may use at most 128 MiB of HBM per device.

v0:
```python
import jax
import jax.numpy as jnp
from jax import lax
from jax.sharding import PartitionSpec as P

HEADS = 12
HD = 64
epsilon = 1e-12
neg_large = -1e30


def layer_norm(value, gain, shift):
    mean_val = jnp.mean(value, axis=-1, keepdims=True)
    centred = value - mean_val
    variance = jnp.mean(centred * centred, axis=-1, keepdims=True)
    return centred * lax.rsqrt(variance + epsilon) * gain + shift


def exact_gelu(value):
    return jax.nn.gelu(value, approximate=False)


def contract_rows(left, right):
    return lax.dot_general(
        left, right, (((0,), (0,)), ((), ())), preferred_element_type=jnp.float32
    )


def contract_cols(left, right):
    return lax.dot_general(
        left, right, (((1,), (1,)), ((), ())), preferred_element_type=jnp.float32
    )


def on_device(
    inputs,
    teacher,
    seq_lengths,
    w_qkv,
    q_bias,
    v_bias,
    w_out,
    out_bias,
    attn_gain,
    attn_shift,
    w_up,
    up_bias,
    w_down,
    down_bias,
    ffn_gain,
    ffn_shift,
):
    tok_rows = inputs.shape[1]
    model_width = inputs.shape[2]
    seq_parts = lax.axis_size("seq")
    group_rows = tok_rows * seq_parts
    heads_dev = HEADS // seq_parts
    head_cols = heads_dev * HD
    block_rows = min(512, group_rows)
    nblocks = group_rows // block_rows
    score_scale = HD ** (-0.5)
    tokens = inputs[0]
    targets = teacher[0].astype(jnp.float32)
    seq_ends = jnp.cumsum(seq_lengths[0])
    all_pos = lax.iota(jnp.int32, group_rows)
    all_seg = jnp.sum((all_pos[:, None] >= seq_ends[None, :]).astype(jnp.int32), axis=1)
    own_seg = lax.dynamic_slice_in_dim(all_seg, lax.axis_index("seq") * tok_rows, tok_rows)
    live_rows = (own_seg < seq_lengths.shape[1]).astype(jnp.float32)
    live_total = lax.psum(seq_ends[-1].astype(jnp.float32), "shard")
    full_qkv, full_q_bias, full_v_bias, full_out, full_out_bias, full_attn_gain, full_attn_shift = (
        lax.all_gather(w_qkv, "shard", axis=0, tiled=True),
        lax.all_gather(q_bias, "shard", axis=0, tiled=True),
        lax.all_gather(v_bias, "shard", axis=0, tiled=True),
        lax.all_gather(w_out, "shard", axis=0, tiled=True),
        lax.all_gather(out_bias, "shard", axis=0, tiled=True),
        lax.all_gather(attn_gain, "shard", axis=0, tiled=True),
        lax.all_gather(attn_shift, "shard", axis=0, tiled=True),
    )
    bias_row = jnp.concatenate([full_q_bias, jnp.zeros_like(full_q_bias), full_v_bias]).astype(
        jnp.float32
    )
    projected = jnp.dot(tokens, full_qkv, preferred_element_type=jnp.float32) + bias_row
    projected = projected.astype(jnp.bfloat16).reshape(tok_rows, 3, seq_parts, head_cols)
    by_heads = lax.all_to_all(projected, "seq", split_axis=2, concat_axis=0, tiled=True)
    queries = by_heads[:, 0, 0]
    keys = by_heads[:, 1, 0]
    values = by_heads[:, 2, 0]

    def block_scores(q_blk, k_head, row_start):
        seg_blk = lax.dynamic_slice_in_dim(all_seg, row_start, block_rows)
        raw = contract_cols(q_blk, k_head) * score_scale
        return jnp.where(seg_blk[:, None] == all_seg[None, :], raw, neg_large)

    def attend(state_in, flat_idx):
        head_idx = flat_idx // nblocks
        row_start = flat_idx % nblocks * block_rows
        q_blk = lax.dynamic_slice(queries, (row_start, head_idx * HD), (block_rows, HD))
        k_head = lax.dynamic_slice_in_dim(keys, head_idx * HD, HD, 1)
        v_head = lax.dynamic_slice_in_dim(values, head_idx * HD, HD, 1)
        scores = block_scores(q_blk, k_head, row_start)
        row_max = jnp.max(scores, axis=1, keepdims=True)
        exp_scores = jnp.exp(scores - row_max)
        row_sum = jnp.sum(exp_scores, axis=1, keepdims=True)
        probs_low = (exp_scores / row_sum).astype(jnp.bfloat16)
        ctx_blk = jnp.dot(probs_low, v_head, preferred_element_type=jnp.float32)
        return (state_in, (ctx_blk.astype(jnp.bfloat16), (row_max + jnp.log(row_sum))[:, 0]))

    flat_ids = jnp.arange(heads_dev * nblocks, dtype=jnp.int32)
    _, (ctx_blocks, lse_blocks) = lax.scan(attend, 0, flat_ids)
    context = jnp.transpose(ctx_blocks.reshape(heads_dev, group_rows, HD), (1, 0, 2)).reshape(
        group_rows, head_cols
    )
    lse_all = lse_blocks.reshape(heads_dev, group_rows)
    merged = lax.all_to_all(
        context.reshape(group_rows, 1, head_cols), "seq", split_axis=0, concat_axis=1, tiled=True
    ).reshape(tok_rows, model_width)
    branch = jnp.dot(merged, full_out, preferred_element_type=jnp.float32) + full_out_bias.astype(
        jnp.float32
    )
    resid_one = tokens.astype(jnp.float32) + branch
    normed, norm_one_back = jax.vjp(
        layer_norm,
        resid_one,
        full_attn_gain.astype(jnp.float32),
        full_attn_shift.astype(jnp.float32),
    )
    full_up, full_up_bias, full_down, full_down_bias, full_ffn_gain, full_ffn_shift = (
        lax.all_gather(w_up, "shard", axis=0, tiled=True),
        lax.all_gather(up_bias, "shard", axis=0, tiled=True),
        lax.all_gather(w_down, "shard", axis=0, tiled=True),
        lax.all_gather(down_bias, "shard", axis=0, tiled=True),
        lax.all_gather(ffn_gain, "shard", axis=0, tiled=True),
        lax.all_gather(ffn_shift, "shard", axis=0, tiled=True),
    )
    normed_low = normed.astype(jnp.bfloat16)
    pre_act = jnp.dot(
        normed_low, full_up, preferred_element_type=jnp.float32
    ) + full_up_bias.astype(jnp.float32)
    activated, gelu_back = jax.vjp(exact_gelu, pre_act)
    act_low = activated.astype(jnp.bfloat16)
    ffn_out = jnp.dot(
        act_low, full_down, preferred_element_type=jnp.float32
    ) + full_down_bias.astype(jnp.float32)
    resid_two = normed + ffn_out
    result, norm_two_back = jax.vjp(
        layer_norm, resid_two, full_ffn_gain.astype(jnp.float32), full_ffn_shift.astype(jnp.float32)
    )
    loss_scale = float(group_rows * lax.axis_size("shard"))
    grad_result = (result - targets) * live_rows[:, None] * (loss_scale / live_total)
    back_qkv, back_out = (
        lax.all_gather(w_qkv, "shard", axis=0, tiled=True),
        lax.all_gather(w_out, "shard", axis=0, tiled=True),
    )
    back_up, back_down = (
        lax.all_gather(w_up, "shard", axis=0, tiled=True),
        lax.all_gather(w_down, "shard", axis=0, tiled=True),
    )
    grad_resid_two, grad_ffn_gain, grad_ffn_shift = norm_two_back(grad_result)
    grad_ffn_low = grad_resid_two.astype(jnp.bfloat16)
    grad_down = contract_rows(act_low, grad_ffn_low)
    grad_down_bias = jnp.sum(grad_ffn_low, axis=0, dtype=jnp.float32)
    grad_act = contract_cols(grad_ffn_low, back_down)
    (grad_pre_full,) = gelu_back(grad_act)
    grad_pre = grad_pre_full.astype(jnp.bfloat16)
    grad_up = contract_rows(normed_low, grad_pre)
    grad_up_bias = jnp.sum(grad_pre, axis=0, dtype=jnp.float32)
    grad_normed = contract_cols(grad_pre, back_up) + grad_resid_two
    grad_resid_one, grad_attn_gain, grad_attn_shift = norm_one_back(grad_normed)
    grad_branch = grad_resid_one.astype(jnp.bfloat16)
    grad_out = contract_rows(merged, grad_branch)
    grad_out_bias = jnp.sum(grad_branch, axis=0, dtype=jnp.float32)
    grad_merged = contract_cols(grad_branch, back_out).astype(jnp.bfloat16)
    grad_context = lax.all_to_all(
        grad_merged.reshape(tok_rows, seq_parts, head_cols),
        "seq",
        split_axis=1,
        concat_axis=0,
        tiled=True,
    ).reshape(group_rows, head_cols)

    def head_back(state_in, head_idx):
        k_head = lax.dynamic_slice_in_dim(keys, head_idx * HD, HD, 1)
        v_head = lax.dynamic_slice_in_dim(values, head_idx * HD, HD, 1)
        lse_head = lax.dynamic_index_in_dim(lse_all, head_idx, 0, keepdims=False)

        def block_back(sums, blk_idx):
            grad_keys, grad_values = sums
            row_start = blk_idx * block_rows
            q_blk = lax.dynamic_slice(queries, (row_start, head_idx * HD), (block_rows, HD))
            dctx_blk = lax.dynamic_slice(grad_context, (row_start, head_idx * HD), (block_rows, HD))
            lse_blk = lax.dynamic_slice_in_dim(lse_head, row_start, block_rows)
            scores = block_scores(q_blk, k_head, row_start)
            probs = jnp.exp(scores - lse_blk[:, None])
            probs_low = probs.astype(jnp.bfloat16)
            grad_probs = contract_cols(dctx_blk, v_head)
            delta = jnp.sum(grad_probs * probs, axis=1, keepdims=True)
            grad_scores = (probs * (grad_probs - delta)).astype(jnp.bfloat16)
            grad_values = grad_values + contract_rows(probs_low, dctx_blk)
            grad_keys = grad_keys + contract_rows(grad_scores, q_blk) * score_scale
            dq_blk = jnp.dot(grad_scores, k_head, preferred_element_type=jnp.float32) * score_scale
            return ((grad_keys, grad_values), dq_blk)

        zero_head = jnp.zeros((group_rows, HD), jnp.float32)
        (grad_keys, grad_values), dq_blocks = lax.scan(
            block_back, (zero_head, zero_head), jnp.arange(nblocks, dtype=jnp.int32)
        )
        return (state_in, (dq_blocks.reshape(group_rows, HD), grad_keys, grad_values))

    _, (grad_q_heads, grad_k_heads, grad_v_heads) = lax.scan(
        head_back, 0, jnp.arange(heads_dev, dtype=jnp.int32)
    )

    def side_by_side(per_head):
        return jnp.transpose(per_head, (1, 0, 2)).reshape(group_rows, head_cols)

    stacked = jnp.stack(
        [side_by_side(grad_q_heads), side_by_side(grad_k_heads), side_by_side(grad_v_heads)], axis=1
    ).astype(jnp.bfloat16)
    grad_proj = lax.all_to_all(
        stacked[:, :, None, :], "seq", split_axis=0, concat_axis=2, tiled=True
    ).reshape(tok_rows, 3 * model_width)
    grad_qkv = contract_rows(tokens, grad_proj)
    grad_q_bias = jnp.sum(grad_proj[:, :model_width], axis=0, dtype=jnp.float32)
    grad_v_bias = jnp.sum(grad_proj[:, 2 * model_width :], axis=0, dtype=jnp.float32)
    grad_inputs = grad_resid_one + contract_cols(grad_proj, back_qkv)
    owned = (
        lax.psum_scatter(grad_qkv, "shard", scatter_dimension=0, tiled=True),
        lax.psum_scatter(grad_q_bias, "shard", scatter_dimension=0, tiled=True),
        lax.psum_scatter(grad_v_bias, "shard", scatter_dimension=0, tiled=True),
        lax.psum_scatter(grad_out, "shard", scatter_dimension=0, tiled=True),
        lax.psum_scatter(grad_out_bias, "shard", scatter_dimension=0, tiled=True),
        lax.psum_scatter(grad_attn_gain, "shard", scatter_dimension=0, tiled=True),
        lax.psum_scatter(grad_attn_shift, "shard", scatter_dimension=0, tiled=True),
        lax.psum_scatter(grad_up, "shard", scatter_dimension=0, tiled=True),
        lax.psum_scatter(grad_up_bias, "shard", scatter_dimension=0, tiled=True),
        lax.psum_scatter(grad_down, "shard", scatter_dimension=0, tiled=True),
        lax.psum_scatter(grad_down_bias, "shard", scatter_dimension=0, tiled=True),
        lax.psum_scatter(grad_ffn_gain, "shard", scatter_dimension=0, tiled=True),
        lax.psum_scatter(grad_ffn_shift, "shard", scatter_dimension=0, tiled=True),
    )
    summed = (
        lax.psum(owned[0].astype(jnp.bfloat16), "seq").astype(jnp.float32),
        lax.psum(owned[1].astype(jnp.bfloat16), "seq").astype(jnp.float32),
        lax.psum(owned[2].astype(jnp.bfloat16), "seq").astype(jnp.float32),
        lax.psum(owned[3].astype(jnp.bfloat16), "seq").astype(jnp.float32),
        lax.psum(owned[4].astype(jnp.bfloat16), "seq").astype(jnp.float32),
        lax.psum(owned[5].astype(jnp.bfloat16), "seq").astype(jnp.float32),
        lax.psum(owned[6].astype(jnp.bfloat16), "seq").astype(jnp.float32),
        lax.psum(owned[7].astype(jnp.bfloat16), "seq").astype(jnp.float32),
        lax.psum(owned[8].astype(jnp.bfloat16), "seq").astype(jnp.float32),
        lax.psum(owned[9].astype(jnp.bfloat16), "seq").astype(jnp.float32),
        lax.psum(owned[10].astype(jnp.bfloat16), "seq").astype(jnp.float32),
        lax.psum(owned[11].astype(jnp.bfloat16), "seq").astype(jnp.float32),
        lax.psum(owned[12].astype(jnp.bfloat16), "seq").astype(jnp.float32),
    )
    return (
        result.astype(jnp.bfloat16)[None],
        grad_inputs.astype(jnp.bfloat16)[None],
        summed[0],
        summed[1],
        summed[2],
        summed[3],
        summed[4],
        summed[5],
        summed[6],
        summed[7],
        summed[8],
        summed[9],
        summed[10],
        summed[11],
        summed[12],
    )


def solution(mesh):
    in_specs = (
        P("shard", "seq", None),
        P("shard", "seq", None),
        P("shard", None),
        P("shard", None),
        P("shard"),
        P("shard"),
        P("shard", None),
        P("shard"),
        P("shard"),
        P("shard"),
        P("shard", None),
        P("shard"),
        P("shard", None),
        P("shard"),
        P("shard"),
        P("shard"),
    )
    out_specs = (
        P("shard", "seq", None),
        P("shard", "seq", None),
        P("shard", None),
        P("shard"),
        P("shard"),
        P("shard", None),
        P("shard"),
        P("shard"),
        P("shard"),
        P("shard", None),
        P("shard"),
        P("shard", None),
        P("shard"),
        P("shard"),
        P("shard"),
    )
    return jax.shard_map(
        on_device, mesh=mesh, in_specs=in_specs, out_specs=out_specs, check_vma=False
    )
```

profile of v0, /device:TPU:0, one launch (start us, length us, event | category | flops | bytes accessed | tf_op | source)
XLA Modules:
  0.0 1513.0 jit_solution(15992502380309811443)
XLA Ops:
  18.1 40.2 %all-reduce.18 = (bf16[768]{0:T(1024)(128)(2,1)S(1)}, bf16[768]{0:T(1024)(128)(2,1)S(1)}, bf16[768]{0:T(1024)(128)(2,1)}, bf16[768]{0:T(1024)(128)(2,1)}, bf16[7...) all-reduce(bf16[768]{0:T(1024)(128)(2,1)S(1)} %dynamic-update-slice, ...), channel_id=1, replica_groups=mesh['seq'=4,'shard'=8] {'shard'}, use_global_device_ids=true, to_apply=%add.1 | all-reduce | flops 6144 | bytes 24576
  58.3 20.2 %all-gather.6.cloned.1.call-done = bf16[768,2304]{1,0:T(8,128)(2,1)} async-done(((bf16[96,2304]{1,0:T(8,128)(2,1)}), bf16[768,2304]{1,0:T(8,128)(2,1)}) %all-gather.6.cloned.1.call-update) | async-done | bytes 3538960 | tf_op jit(solution)/shard_map/all_gather | solution.py:71
  98.2 39.1 %all-to-all-done = bf16[768,3,4,192]{0,3,1,2:T(8,128)(2,1)S(1)} async-done(((bf16[768,3,4,192]{0,3,1,2:T(8,128)(2,1)}), bf16[768,3,4,192]{0,3,1,2:T(8,128)(2,1)S(1)}, u32[]{:S(2)}, u32[]{:S(2)}) %all-to-all-start) | async-done | bytes 3538976 | tf_op jit(solution)/shard_map/all_to_all | solution.py:84
  142.8 189.0 %while.45 = (s32[]{:T(128)}, bf16[18,512,64]{1,2,0:T(8,128)(2,1)S(1)}, f32[18,512]{1,0:T(8,128)}, s32[18]{0:T(128)S(1)}, s32[3072]{0:T(1024)S(1)}, /*index=5*/bf...) while((s32[]{:T(128)}, ...), condition=%wide.region_5.6_spmd, body=%wide.region_2.0_spmd.sunk | while | flops 416841216 | bytes 20684696 | solution.py:109
  345.3 20.4 %psum.98 = f32[]{:T(128)} all-reduce(f32[]{:T(128)} %bitcast.27), channel_id=1, replica_groups=mesh['seq'=4,'shard'=8] {'shard'}, use_global_device_ids=true, to_apply=%region_10.11 | all-reduce | flops 1 | bytes 8 | tf_op jit(solution)/shard_map/psum | solution.py:69
  367.7 25.9 %all-gather = bf16[8,1,384]{2,1,0:T(2,128)(2,1)S(1)} all-gather(bf16[1,1,384]{2,1,0:T(2,128)(2,1)S(1)} %reshape.280), channel_id=1, replica_groups=mesh['seq'=4,'shard'=8] {'shard'}, dimensions={0}, use_global_device_ids=true | all-gather | bytes 6912 | tf_op jit(solution)/shard_map/all_gather | solution.py:129
  416.9 28.7 %multiply_convert_fusion.1 = (bf16[768,3072]{1,0:T(8,128)(2,1)}, f32[768,3072]{1,0:T(8,128)}, f32[768,3072]{1,0:T(8,128)}) fusion(f32[3072]{0:T(1024)} %bitcast.163, bf16[768,3072]{1,0:T(8,128)(2,1)} %all-gather.10.cloned.1.call-done, f32[768,768]{0,1:T(8,128)S(1)} %get-tuple-element.713, f32[768]{0:T(1024)} %convert_element_type.205, ...), kind=kOutput, calls=%fused_computation.39 | convolution fusion | flops 3782541312 | bytes 30695424 | tf_op jit(solution)/shard_map/dot_general | solution.py:136
  445.6 7.7 fusion.47
  460.0 13.5 convert_reduce_fusion
  473.6 7.6 multiply_reduce_fusion.2
  493.7 11.8 all-to-all-done.2
  507.1 362.0 %while.47 = (s32[]{:T(128)}, bf16[3,3072,64]{1,2,0:T(8,128)(2,1)}, bf16[3,3072,64]{1,2,0:T(8,128)(2,1)}, bf16[3,3072,64]{1,2,0:T(8,128)(2,1)}, s32[3]{0:T(128)S(...) while((s32[]{:T(128)}, bf16[3,3072,64]{1,2,0:T(8,128)(2,1)}, ...), condition=%wide.region_19.20_spmd, body=%wide.region_15.19_spmd.sunk | while | flops 1023376896 | bytes 123100080 | solution.py:209
  516.5 109.1 %while.48 = (s32[]{:T(128)}, f32[3072,64]{0,1:T(8,128)}, f32[3072,64]{0,1:T(8,128)}, bf16[6,512,64]{1,2,0:T(8,128)(2,1)S(1)}, s32[6]{0:T(128)}, /*index=5*/s32[3...) while((s32[]{:T(128)}, f32[3072,64]{0,1:T(8,128)}, ...), condition=%wide.region_18.18_spmd.clone, body=%wide.region_16.17_spmd.clone.sunk | while | flops 1023376896 | bytes 109607288 | solution.py:204
  637.3 108.8 %while.48 = (s32[]{:T(128)}, f32[3072,64]{0,1:T(8,128)}, f32[3072,64]{0,1:T(8,128)}, bf16[6,512,64]{1,2,0:T(8,128)(2,1)S(1)}, s32[6]{0:T(128)}, /*index=5*/s32[3...) while((s32[]{:T(128)}, f32[3072,64]{0,1:T(8,128)}, ...), condition=%wide.region_18.18_spmd.clone, body=%wide.region_16.17_spmd.clone.sunk | while | flops 1023376896 | bytes 109607288 | solution.py:204
  757.9 108.8 %while.48 = (s32[]{:T(128)}, f32[3072,64]{0,1:T(8,128)}, f32[3072,64]{0,1:T(8,128)}, bf16[6,512,64]{1,2,0:T(8,128)(2,1)S(1)}, s32[6]{0:T(128)}, /*index=5*/s32[3...) while((s32[]{:T(128)}, f32[3072,64]{0,1:T(8,128)}, ...), condition=%wide.region_18.18_spmd.clone, body=%wide.region_16.17_spmd.clone.sunk | while | flops 1023376896 | bytes 109607288 | solution.py:204
  878.3 77.3 %all_to_all.63 = bf16[3072,3,1,192]{3,1,2,0:T(4,128)(2,1)} all-to-all(bf16[3072,3,1,192]{3,1,2,0:T(4,128)(2,1)} %copy.198), channel_id=1, replica_groups=mesh['seq'=4,'shard'=8] {'seq'}, dimensions={0} | all-to-all | bytes 7077888 | tf_op jit(solution)/shard_map/all_to_all | solution.py:219
  955.6 10.5 copy.208
  973.4 8.1 copy.209
  983.1 9.7 fusion.37
  994.1 8.8 fusion.49
  1007.5 99.3 %reduce-scatter.13.cloned.1.call-done = f32[96,2304]{1,0:T(8,128)} async-done(((f32[768,2304]{1,0:T(8,128)}), f32[96,2304]{1,0:T(8,128)}) %reduce-scatter.13.cloned.1.call-update) | async-done | bytes 884752
  1109.0 164.3 %reduce-scatter.9.cloned.1.call-done = f32[96,3072]{1,0:T(8,128)} async-done(((f32[768,3072]{1,0:T(8,128)}), f32[96,3072]{1,0:T(8,128)}) %reduce-scatter.9.cloned.1.call-update) | async-done | bytes 1179664 | tf_op jit(solution)/shard_map/reduce_scatter | solution.py:234
  1275.5 164.5 %reduce-scatter.11.cloned.1.call-done = f32[384,768]{1,0:T(8,128)} async-done(((f32[3072,768]{1,0:T(8,128)}), f32[384,768]{1,0:T(8,128)}) %reduce-scatter.11.cloned.1.call-update) | async-done | bytes 1179664 | tf_op jit(solution)/shard_map/reduce_scatter | solution.py:236
  1451.6 36.1 %all-reduce.17 = (bf16[768]{0:T(1024)(128)(2,1)S(1)}, bf16[768]{0:T(1024)(128)(2,1)S(1)}, bf16[768]{0:T(1024)(128)(2,1)S(1)}, bf16[768]{0:T(1024)(128)(2,1)S(1)}...) all-reduce(f32[768]{0:T(1024)S(1)} %get-tuple-element.594, ...), channel_id=3, replica_groups=mesh['seq'=4,'shard'=8] {'shard'}, use_global_device_ids=true, to_apply=%region_23.24.clone | all-reduce | flops 9216 | bytes 55296
  (723 shorter events, 643.8 us)
Async XLA Ops:
  7.2 71.4 %all-gather.6.cloned.1.call-start = ((), (), s32[]{:S(2)}) async-start(), calls=%async_computation.8 | async-start | bytes 3981312 | tf_op jit(solution)/shard_map/all_gather | solution.py:71
  7.9 404.4 %all-gather.8.cloned.1.call-start = ((), (), s32[]{:S(2)}) async-start(), calls=%async_computation.9 | async-start | bytes 1327104 | tf_op jit(solution)/shard_map/all_gather | solution.py:74
  8.7 408.2 %all-gather.10.cloned.1.call-start = ((), (), s32[]{:S(2)}) async-start(), calls=%async_computation.10 | async-start | bytes 5308416 | tf_op jit(solution)/shard_map/all_gather | solution.py:128
  92.3 45.0 %all-to-all-start = ((bf16[768,3,4,192]{0,3,1,2:T(8,128)(2,1)}), bf16[768,3,4,192]{0,3,1,2:T(8,128)(2,1)S(1)}, u32[]{:S(2)}, u32[]{:S(2)}) async-start(bf16[768,3,4,192]{0,3,1,2:T(8,128)(2,1)} %copy.178), calls=%async_computation | async-start | bytes 7077888 | tf_op jit(solution)/shard_map/all_to_all | solution.py:84
  96.2 349.5 %all-gather.12.cloned.1.call-start = ((), (), s32[]{:S(2)}) async-start(), calls=%async_computation.11 | async-start | bytes 5308416 | tf_op jit(solution)/shard_map/all_gather | solution.py:130
  336.7 28.9 %copy-start.16 = (bf16[1,768,768]{2,1,0:T(8,128)(2,1)S(1)}, bf16[1,768,768]{2,1,0:T(8,128)(2,1)}, u32[]{:S(2)}) copy-start(bf16[1,768,768]{2,1,0:T(8,128)(2,1)} %param.22) | copy-start | bytes 3538948
  339.6 28.1 %copy-start.44 = (bf16[384]{0:T(512)(128)(2,1)S(1)}, bf16[384]{0:T(512)(128)(2,1)}, u32[]{:S(2)}) copy-start(bf16[384]{0:T(512)(128)(2,1)} %param.33) | copy-start | bytes 2308
  339.6 54.6 %copy-start.43 = (bf16[768]{0:T(1024)(128)(2,1)S(1)}, bf16[768]{0:T(1024)(128)(2,1)}, u32[]{:S(2)}) copy-start(bf16[768]{0:T(1024)(128)(2,1)} %get-tuple-element.669) | copy-start | bytes 4612
  339.6 54.7 %copy-start.42 = (bf16[768]{0:T(1024)(128)(2,1)S(1)}, bf16[768]{0:T(1024)(128)(2,1)}, u32[]{:S(2)}) copy-start(bf16[768]{0:T(1024)(128)(2,1)} %get-tuple-element.670) | copy-start | bytes 4612
  339.6 55.2 %copy-start.41 = (bf16[768]{0:T(1024)(128)(2,1)S(1)}, bf16[768]{0:T(1024)(128)(2,1)}, u32[]{:S(2)}) copy-start(bf16[768]{0:T(1024)(128)(2,1)} %get-tuple-element.671) | copy-start | bytes 4612
  339.6 55.8 %copy-start.15 = (bf16[1,768,768]{2,1,0:T(8,128)(2,1)S(1)}, bf16[1,768,768]{2,1,0:T(8,128)(2,1)}, u32[]{:S(2)}) copy-start(bf16[1,768,768]{2,1,0:T(8,128)(2,1)} %param.23) | copy-start | bytes 3538948
  339.6 60.3 %all-to-all-start.1 = ((bf16[4,2,73728]{2,1,0:T(2,128)(2,1)}), bf16[4,2,73728]{2,1,0:T(2,128)(2,1)}, u32[]{:S(2)}, u32[]{:S(2)}) async-start(bf16[4,2,73728]{2,1,0:T(2,128)(2,1)} %reshape.310), calls=%async_computation.1 | async-start | bytes 2359296 | tf_op jit(solution)/shard_map/all_to_all | solution.py:114
  365.7 31.6 %copy-start.40 = (bf16[768]{0:T(1024)(128)(2,1)S(1)}, bf16[768]{0:T(1024)(128)(2,1)}, u32[]{:S(2)}) copy-start(bf16[768]{0:T(1024)(128)(2,1)} %get-tuple-element.673) | copy-start | bytes 4612
  365.7 32.2 %copy-start.39 = (bf16[768]{0:T(1024)(128)(2,1)S(1)}, bf16[768]{0:T(1024)(128)(2,1)}, u32[]{:S(2)}) copy-start(bf16[768]{0:T(1024)(128)(2,1)} %get-tuple-element.674) | copy-start | bytes 4612
  415.2 66.0 %copy-start.10 = (f32[768,768]{0,1:T(8,128)}, f32[768,768]{0,1:T(8,128)S(1)}, u32[]{:S(2)}) copy-start(f32[768,768]{0,1:T(8,128)S(1)} %get-tuple-element.713) | copy-start | bytes 7077892
  415.2 66.0 %copy-start.22 = (f32[768]{0:T(1024)}, f32[768]{0:T(1024)S(1)}, u32[]{:S(2)}) copy-start(f32[768]{0:T(1024)S(1)} %broadcast_multiply_fusion.1) | copy-start | bytes 9220
  486.0 19.4 %all-to-all-start.2 = ((bf16[768,4,192]{0,2,1:T(8,128)(2,1)}), bf16[768,4,192]{0,2,1:T(8,128)(2,1)S(1)}, u32[]{:S(2)}, u32[]{:S(2)}) async-start(bf16[768,4,192]{0,2,1:T(8,128)(2,1)} %bitcast.160), calls=%async_computation.2 | async-start | bytes 2359296 | tf_op jit(solution)/shard_map/all_to_all | solution.py:173
  489.6 516.2 %reduce-scatter.7.cloned.1.call-start = ((), (), s32[]{:S(2)}) async-start(), calls=%async_computation.12 | async-start | bytes 2654208 | tf_op jit(solution)/shard_map/reduce_scatter | solution.py:230
  493.6 613.2 %reduce-scatter.13.cloned.1.call-start = ((), (), s32[]{:S(2)}) async-start(), calls=%async_computation.15 | async-start | bytes 7962624
  981.5 291.9 %reduce-scatter.9.cloned.1.call-start = ((), (), s32[]{:S(2)}) async-start(), calls=%async_computation.13 | async-start | bytes 10616832 | tf_op jit(solution)/shard_map/reduce_scatter | solution.py:234
  992.9 447.1 %reduce-scatter.11.cloned.1.call-start = ((), (), s32[]{:S(2)}) async-start(), calls=%async_computation.14 | async-start | bytes 10616832 | tf_op jit(solution)/shard_map/reduce_scatter | solution.py:236
  1002.9 496.0 %all-reduce.23.cloned.1.call-start = ((), (), s32[]{:S(2)}) async-start(), calls=%async_computation.16 | async-start | bytes 3833856 | tf_op jit(solution)/shard_map/psum | solution.py:242
  1109.0 333.2 %copy-start.8 = (bf16[768,3,4,1,192]{0,4,2,1,3:T(8,128)(2,1)S(1)}, bf16[768,3,4,1,192]{0,4,2,1,3:T(8,128)(2,1)}, u32[]{:S(2)}) copy-start(bf16[768,3,4,1,192]{0,4,2,1,3:T(8,128)(2,1)} %copy-done.7) | copy-start | bytes 10616836
  1109.0 333.2 %copy-start.32 = (f32[768]{0:T(1024)S(1)}, f32[768]{0:T(1024)}, u32[]{:S(2)}) copy-start(f32[768]{0:T(1024)} %copy-done.31) | copy-start | bytes 9220
  (116 other events, 393.1 us)
Sparse Core Ops, SparseCore 0:
  10.2 68.2 all-gather.5
  80.7 39.6 all-gather.7
  122.6 78.6 all-gather.9
  203.4 78.1 all-gather.11
  493.7 66.7 reduce-scatter.6
  981.6 125.1 reduce-scatter.12
  1110.8 162.5 reduce-scatter.8
  1277.4 162.5 reduce-scatter.10
  1444.0 48.2 all-reduce.22
where the time goes:
time: 1530 us; the launch traced here: 1510 us
  waiting for transfers between devices  502 us (33%)
  matrix products  437 us (29%)
  blocking collectives  206 us (13%)
  local copies, waits for them, and re-layouts  199 us (13%)
  other arithmetic  82.2 us (5%)
  loops' own time  57.2 us (4%)
  between operations  18.3 us (1%)
    dot_general x58, matrix products, contract_cols(): lax.dot_general(left, right, (((1,), (1,)), ((), ())), preferred_element_...  184 us
    reduce_scatter x1, waiting for transfers between devices, on_device(): lax.psum_scatter(grad_down, 'shard', scatter_dimension=0, tiled=True)  164 us
    reduce_scatter x1, waiting for transfers between devices, on_device(): lax.psum_scatter(grad_up, 'shard', scatter_dimension=0, tiled=True)  164 us
    dot_general x40, matrix products, contract_rows(): lax.dot_general(left, right, (((0,), (0,)), ((), ())), preferred_element_...  111 us
    unnamed x10, waiting for transfers between devices  102 us
    all_to_all x1, blocking collectives, on_device(): lax.all_to_all(stacked[:, :, None, :], 'seq', split_axis=0, concat_axis=2...  77.3 us
    unnamed x2, blocking collectives  76.4 us
    dot_general x18, matrix products, attend(): ctx_blk = jnp.dot(probs_low, v_head, preferred_element_type=jnp.float32)  50.9 us
  transfers between devices with their start and end apart: 12, of which 6 were waited for; matrix products, arithmetic and copies ran while one was open for 43% of the time, Pallas kernels for 0%

commit v1 on v0

--- a/solution.py
+++ b/solution.py
@@ -7,6 +7,18 @@
 HD = 64
 epsilon = 1e-12
 neg_large = -1e30
+
+
+def fix_face(work_x, chip_axis="seq"):
+    return jnp.concatenate(
+        lax.all_to_all(
+            jnp.stack(jnp.split(work_x, lax.axis_size(chip_axis), 0)),
+            split_axis=0,
+            axis_name=chip_axis,
+            concat_axis=0,
+        ),
+        2,
+    )
 
 
 def layer_norm(value, gain, shift):
@@ -216,9 +228,7 @@
     stacked = jnp.stack(
         [side_by_side(grad_q_heads), side_by_side(grad_k_heads), side_by_side(grad_v_heads)], axis=1
     ).astype(jnp.bfloat16)
-    grad_proj = lax.all_to_all(
-        stacked[:, :, None, :], "seq", split_axis=0, concat_axis=2, tiled=True
-    ).reshape(tok_rows, 3 * model_width)
+    grad_proj = fix_face(stacked[:, :, None, :]).reshape(tok_rows, 3 * model_width)
     grad_qkv = contract_rows(tokens, grad_proj)
     grad_q_bias = jnp.sum(grad_proj[:, :model_width], axis=0, dtype=jnp.float32)
     grad_v_bias = jnp.sum(grad_proj[:, 2 * model_width :], axis=0, dtype=jnp.float32)

time: 1530 us -> 1470 us (0.961)
  blocking collectives: 206 us -> 172 us
  local copies, waits for them, and re-layouts: 199 us -> 179 us
    all_to_all x1, blocking collectives: 77.3 us -> 43.7 us  [fix_face(): lax.all_to_all(jnp.stack(jnp.split(work_x, lax.axis_size(chip_axis), 0)),...]
    unnamed x126 -> x116, local copies, waits for them, and re-layouts: 43.1 us -> 40.7 us
  transfers between devices with their start and end apart: 12 -> 12, of which waited for: 6 -> 6; matrix products, arithmetic and copies ran while one was open for 43% -> 44% of each run, Pallas kernels for 0% -> 0%
where the time goes in v1:
time: 1470 us; the launch traced here: 1460 us
  waiting for transfers between devices  500 us (34%)
  matrix products  440 us (30%)
  local copies, waits for them, and re-layouts  179 us (12%)
  blocking collectives  172 us (12%)
  other arithmetic  82.7 us (6%)
  loops' own time  57.2 us (4%)
  between operations  17.9 us (1%)
    dot_general x58, matrix products, contract_cols(): lax.dot_general(left, right, (((1,), (1,)), ((), ())), preferred_element_...  184 us
    reduce_scatter x1, waiting for transfers between devices, on_device(): lax.psum_scatter(grad_down, 'shard', scatter_dimension=0, tiled=True)  164 us
    reduce_scatter x1, waiting for transfers between devices, on_device(): lax.psum_scatter(grad_up, 'shard', scatter_dimension=0, tiled=True)  164 us
    dot_general x40, matrix products, contract_rows(): lax.dot_general(left, right, (((0,), (0,)), ((), ())), preferred_element_...  114 us
    unnamed x10, waiting for transfers between devices  100 us
    unnamed x2, blocking collectives  76.4 us
    dot_general x18, matrix products, attend(): ctx_blk = jnp.dot(probs_low, v_head, preferred_element_type=jnp.float32)  50.9 us
    dot_general x18, matrix products, block_back(): jnp.dot(grad_scores, k_head, preferred_element_type=jnp.float32)  45 us
  transfers between devices with their start and end apart: 12, of which 6 were waited for; matrix products, arithmetic and copies ran while one was open for 44% of the time, Pallas kernels for 0%

profile of v1, /device:TPU:0, one launch (start us, length us, event | category | flops | bytes accessed | tf_op | source)
XLA Modules:
  0.0 1461.4 jit_solution(13964920148770104812)
XLA Ops:
  18.1 40.2 %all-reduce.18 = (bf16[768]{0:T(1024)(128)(2,1)S(1)}, bf16[768]{0:T(1024)(128)(2,1)S(1)}, bf16[768]{0:T(1024)(128)(2,1)}, bf16[768]{0:T(1024)(128)(2,1)}, bf16[7...) all-reduce(bf16[768]{0:T(1024)(128)(2,1)S(1)} %dynamic-update-slice, ...), channel_id=1, replica_groups=mesh['seq'=4,'shard'=8] {'shard'}, use_global_device_ids=true, to_apply=%add.1 | all-reduce | flops 6144 | bytes 24576
  58.3 20.2 %all-gather.6.cloned.1.call-done = bf16[768,2304]{1,0:T(8,128)(2,1)} async-done(((bf16[96,2304]{1,0:T(8,128)(2,1)}), bf16[768,2304]{1,0:T(8,128)(2,1)}) %all-gather.6.cloned.1.call-update) | async-done | bytes 3538960 | tf_op jit(solution)/shard_map/all_gather | solution.py:83
  78.5 7.1 add_convert_fusion.1
  98.2 39.1 %all-to-all-done = bf16[768,3,4,192]{0,3,1,2:T(8,128)(2,1)S(1)} async-done(((bf16[768,3,4,192]{0,3,1,2:T(8,128)(2,1)}), bf16[768,3,4,192]{0,3,1,2:T(8,128)(2,1)S(1)}, u32[]{:S(2)}, u32[]{:S(2)}) %all-to-all-start) | async-done | bytes 3538976 | tf_op jit(solution)/shard_map/all_to_all | solution.py:96
  142.7 189.1 %while.45 = (s32[]{:T(128)}, bf16[18,512,64]{1,2,0:T(8,128)(2,1)S(1)}, f32[18,512]{1,0:T(8,128)}, s32[18]{0:T(128)S(1)}, s32[3072]{0:T(1024)S(1)}, /*index=5*/bf...) while((s32[]{:T(128)}, ...), condition=%wide.region_5.6_spmd, body=%wide.region_2.0_spmd.sunk | while | flops 416841216 | bytes 20684696 | solution.py:121
  345.3 20.4 %psum.98 = f32[]{:T(128)} all-reduce(f32[]{:T(128)} %bitcast.27), channel_id=1, replica_groups=mesh['seq'=4,'shard'=8] {'shard'}, use_global_device_ids=true, to_apply=%region_10.11 | all-reduce | flops 1 | bytes 8 | tf_op jit(solution)/shard_map/psum | solution.py:81
  367.7 25.9 %all-gather = bf16[8,1,384]{2,1,0:T(2,128)(2,1)S(1)} all-gather(bf16[1,1,384]{2,1,0:T(2,128)(2,1)S(1)} %reshape.239), channel_id=1, replica_groups=mesh['seq'=4,'shard'=8] {'shard'}, dimensions={0}, use_global_device_ids=true | all-gather | bytes 6912 | tf_op jit(solution)/shard_map/all_gather | solution.py:141
  416.6 28.8 %multiply_convert_fusion.1 = (bf16[768,3072]{1,0:T(8,128)(2,1)}, f32[768,3072]{1,0:T(8,128)}, f32[768,3072]{1,0:T(8,128)}) fusion(f32[3072]{0:T(1024)} %bitcast.169, bf16[768,3072]{1,0:T(8,128)(2,1)} %all-gather.10.cloned.1.call-done, f32[768,768]{0,1:T(8,128)S(1)} %get-tuple-element.649, f32[768]{0:T(1024)} %convert_element_type.198, ...), kind=kOutput, calls=%fused_computation.39 | convolution fusion | flops 3782541312 | bytes 30695424 | tf_op jit(solution)/shard_map/dot_general | solution.py:148
  445.4 8.0 fusion.47
  459.9 13.6 convert_reduce_fusion
  473.5 7.6 multiply_reduce_fusion.2
  493.6 11.8 all-to-all-done.2
  507.1 362.1 %while.47 = (s32[]{:T(128)}, bf16[3,3072,64]{1,2,0:T(8,128)(2,1)}, bf16[3,3072,64]{1,2,0:T(8,128)(2,1)}, bf16[3,3072,64]{1,2,0:T(8,128)(2,1)}, s32[3]{0:T(128)S(...) while((s32[]{:T(128)}, bf16[3,3072,64]{1,2,0:T(8,128)(2,1)}, ...), condition=%wide.region_19.20_spmd, body=%wide.region_15.19_spmd.sunk | while | flops 1023376896 | bytes 123100080 | solution.py:221
  516.4 109.1 %while.48 = (s32[]{:T(128)}, f32[3072,64]{0,1:T(8,128)}, f32[3072,64]{0,1:T(8,128)}, bf16[6,512,64]{1,2,0:T(8,128)(2,1)S(1)}, s32[6]{0:T(128)}, /*index=5*/s32[3...) while((s32[]{:T(128)}, f32[3072,64]{0,1:T(8,128)}, ...), condition=%wide.region_18.18_spmd.clone, body=%wide.region_16.17_spmd.clone.sunk | while | flops 1023376896 | bytes 109607288 | solution.py:216
  637.3 108.8 %while.48 = (s32[]{:T(128)}, f32[3072,64]{0,1:T(8,128)}, f32[3072,64]{0,1:T(8,128)}, bf16[6,512,64]{1,2,0:T(8,128)(2,1)S(1)}, s32[6]{0:T(128)}, /*index=5*/s32[3...) while((s32[]{:T(128)}, f32[3072,64]{0,1:T(8,128)}, ...), condition=%wide.region_18.18_spmd.clone, body=%wide.region_16.17_spmd.clone.sunk | while | flops 1023376896 | bytes 109607288 | solution.py:216
  757.9 108.8 %while.48 = (s32[]{:T(128)}, f32[3072,64]{0,1:T(8,128)}, f32[3072,64]{0,1:T(8,128)}, bf16[6,512,64]{1,2,0:T(8,128)(2,1)S(1)}, s32[6]{0:T(128)}, /*index=5*/s32[3...) while((s32[]{:T(128)}, f32[3072,64]{0,1:T(8,128)}, ...), condition=%wide.region_18.18_spmd.clone, body=%wide.region_16.17_spmd.clone.sunk | while | flops 1023376896 | bytes 109607288 | solution.py:216
  872.2 43.7 %all_to_all.53 = bf16[4,768,3,1,192]{1,4,2,3,0:T(8,128)(2,1)S(1)} all-to-all(bf16[4,768,3,1,192]{1,4,2,3,0:T(8,128)(2,1)S(1)} %pad_maximum_fusion.1), channel_id=1, replica_groups=mesh['seq'=4,'shard'=8] {'seq'}, dimensions={0} | all-to-all | bytes 7077888 | tf_op jit(solution)/shard_map/all_to_all | solution.py:14
  922.0 8.1 copy.146
  930.8 10.9 fusion.37
  941.7 10.3 fusion.49
  957.4 98.0 %reduce-scatter.13.cloned.1.call-done = f32[96,2304]{1,0:T(8,128)} async-done(((f32[768,2304]{1,0:T(8,128)}), f32[96,2304]{1,0:T(8,128)}) %reduce-scatter.13.cloned.1.call-update) | async-done | bytes 884752
  1057.6 164.3 %reduce-scatter.9.cloned.1.call-done = f32[96,3072]{1,0:T(8,128)} async-done(((f32[768,3072]{1,0:T(8,128)}), f32[96,3072]{1,0:T(8,128)}) %reduce-scatter.9.cloned.1.call-update) | async-done | bytes 1179664 | tf_op jit(solution)/shard_map/reduce_scatter | solution.py:244
  1224.1 164.5 %reduce-scatter.11.cloned.1.call-done = f32[384,768]{1,0:T(8,128)} async-done(((f32[3072,768]{1,0:T(8,128)}), f32[384,768]{1,0:T(8,128)}) %reduce-scatter.11.cloned.1.call-update) | async-done | bytes 1179664 | tf_op jit(solution)/shard_map/reduce_scatter | solution.py:246
  1400.2 36.1 %all-reduce.17 = (bf16[768]{0:T(1024)(128)(2,1)S(1)}, bf16[768]{0:T(1024)(128)(2,1)S(1)}, bf16[768]{0:T(1024)(128)(2,1)S(1)}, bf16[768]{0:T(1024)(128)(2,1)S(1)}...) all-reduce(f32[768]{0:T(1024)S(1)} %get-tuple-element.526, ...), channel_id=3, replica_groups=mesh['seq'=4,'shard'=8] {'shard'}, use_global_device_ids=true, to_apply=%region_23.24.clone | all-reduce | flops 9216 | bytes 55296
  (713 shorter events, 628.0 us)
Async XLA Ops:
  7.2 71.4 %all-gather.6.cloned.1.call-start = ((), (), s32[]{:S(2)}) async-start(), calls=%async_computation.8 | async-start | bytes 3981312 | tf_op jit(solution)/shard_map/all_gather | solution.py:83
  7.9 404.1 %all-gather.8.cloned.1.call-start = ((), (), s32[]{:S(2)}) async-start(), calls=%async_computation.9 | async-start | bytes 1327104 | tf_op jit(solution)/shard_map/all_gather | solution.py:86
  8.7 407.9 %all-gather.10.cloned.1.call-start = ((), (), s32[]{:S(2)}) async-start(), calls=%async_computation.10 | async-start | bytes 5308416 | tf_op jit(solution)/shard_map/all_gather | solution.py:140
  92.3 45.0 %all-to-all-start = ((bf16[768,3,4,192]{0,3,1,2:T(8,128)(2,1)}), bf16[768,3,4,192]{0,3,1,2:T(8,128)(2,1)S(1)}, u32[]{:S(2)}, u32[]{:S(2)}) async-start(bf16[768,3,4,192]{0,3,1,2:T(8,128)(2,1)} %copy.118), calls=%async_computation | async-start | bytes 7077888 | tf_op jit(solution)/shard_map/all_to_all | solution.py:96
  96.2 349.2 %all-gather.12.cloned.1.call-start = ((), (), s32[]{:S(2)}) async-start(), calls=%async_computation.11 | async-start | bytes 5308416 | tf_op jit(solution)/shard_map/all_gather | solution.py:142
  336.7 28.9 %copy-start.11 = (bf16[1,768,768]{2,1,0:T(8,128)(2,1)S(1)}, bf16[1,768,768]{2,1,0:T(8,128)(2,1)}, u32[]{:S(2)}) copy-start(bf16[1,768,768]{2,1,0:T(8,128)(2,1)} %param.22) | copy-start | bytes 3538948
  339.6 28.1 %copy-start.39 = (bf16[384]{0:T(512)(128)(2,1)S(1)}, bf16[384]{0:T(512)(128)(2,1)}, u32[]{:S(2)}) copy-start(bf16[384]{0:T(512)(128)(2,1)} %param.33) | copy-start | bytes 2308
  339.6 54.6 %copy-start.38 = (bf16[768]{0:T(1024)(128)(2,1)S(1)}, bf16[768]{0:T(1024)(128)(2,1)}, u32[]{:S(2)}) copy-start(bf16[768]{0:T(1024)(128)(2,1)} %get-tuple-element.601) | copy-start | bytes 4612
  339.6 54.6 %copy-start.37 = (bf16[768]{0:T(1024)(128)(2,1)S(1)}, bf16[768]{0:T(1024)(128)(2,1)}, u32[]{:S(2)}) copy-start(bf16[768]{0:T(1024)(128)(2,1)} %get-tuple-element.602) | copy-start | bytes 4612
  339.6 55.2 %copy-start.36 = (bf16[768]{0:T(1024)(128)(2,1)S(1)}, bf16[768]{0:T(1024)(128)(2,1)}, u32[]{:S(2)}) copy-start(bf16[768]{0:T(1024)(128)(2,1)} %get-tuple-element.603) | copy-start | bytes 4612
  339.6 55.8 %copy-start.10 = (bf16[1,768,768]{2,1,0:T(8,128)(2,1)S(1)}, bf16[1,768,768]{2,1,0:T(8,128)(2,1)}, u32[]{:S(2)}) copy-start(bf16[1,768,768]{2,1,0:T(8,128)(2,1)} %param.23) | copy-start | bytes 3538948
  339.6 59.9 %all-to-all-start.1 = ((bf16[4,2,73728]{2,1,0:T(2,128)(2,1)}), bf16[4,2,73728]{2,1,0:T(2,128)(2,1)}, u32[]{:S(2)}, u32[]{:S(2)}) async-start(bf16[4,2,73728]{2,1,0:T(2,128)(2,1)} %reshape.269), calls=%async_computation.1 | async-start | bytes 2359296 | tf_op jit(solution)/shard_map/all_to_all | solution.py:126
  365.7 31.4 %copy-start.35 = (bf16[768]{0:T(1024)(128)(2,1)S(1)}, bf16[768]{0:T(1024)(128)(2,1)}, u32[]{:S(2)}) copy-start(bf16[768]{0:T(1024)(128)(2,1)} %get-tuple-element.605) | copy-start | bytes 4612
  365.7 31.9 %copy-start.34 = (bf16[768]{0:T(1024)(128)(2,1)S(1)}, bf16[768]{0:T(1024)(128)(2,1)}, u32[]{:S(2)}) copy-start(bf16[768]{0:T(1024)(128)(2,1)} %get-tuple-element.606) | copy-start | bytes 4612
  414.8 66.3 %copy-start.8 = (f32[768,768]{0,1:T(8,128)}, f32[768,768]{0,1:T(8,128)S(1)}, u32[]{:S(2)}) copy-start(f32[768,768]{0,1:T(8,128)S(1)} %get-tuple-element.649) | copy-start | bytes 7077892
  414.8 66.3 %copy-start.17 = (f32[768]{0:T(1024)}, f32[768]{0:T(1024)S(1)}, u32[]{:S(2)}) copy-start(f32[768]{0:T(1024)S(1)} %broadcast_multiply_fusion.1) | copy-start | bytes 9220
  459.0 14.5 slice-start
  486.0 19.4 %all-to-all-start.2 = ((bf16[768,4,192]{0,2,1:T(8,128)(2,1)}), bf16[768,4,192]{0,2,1:T(8,128)(2,1)S(1)}, u32[]{:S(2)}, u32[]{:S(2)}) async-start(bf16[768,4,192]{0,2,1:T(8,128)(2,1)} %bitcast.166), calls=%async_computation.2 | async-start | bytes 2359296 | tf_op jit(solution)/shard_map/all_to_all | solution.py:185
  489.6 466.2 %reduce-scatter.7.cloned.1.call-start = ((), (), s32[]{:S(2)}) async-start(), calls=%async_computation.12 | async-start | bytes 2654208 | tf_op jit(solution)/shard_map/reduce_scatter | solution.py:240
  493.6 561.8 %reduce-scatter.13.cloned.1.call-start = ((), (), s32[]{:S(2)}) async-start(), calls=%async_computation.15 | async-start | bytes 7962624
  930.1 291.9 %reduce-scatter.9.cloned.1.call-start = ((), (), s32[]{:S(2)}) async-start(), calls=%async_computation.13 | async-start | bytes 10616832 | tf_op jit(solution)/shard_map/reduce_scatter | solution.py:244
  941.7 446.9 %reduce-scatter.11.cloned.1.call-start = ((), (), s32[]{:S(2)}) async-start(), calls=%async_computation.14 | async-start | bytes 10616832 | tf_op jit(solution)/shard_map/reduce_scatter | solution.py:246
  952.1 495.4 %all-reduce.23.cloned.1.call-start = ((), (), s32[]{:S(2)}) async-start(), calls=%async_computation.16 | async-start | bytes 3833856 | tf_op jit(solution)/shard_map/psum | solution.py:252
  1057.6 333.2 %copy-start.27 = (f32[768]{0:T(1024)S(1)}, f32[768]{0:T(1024)}, u32[]{:S(2)}) copy-start(f32[768]{0:T(1024)} %copy-done.26) | copy-start | bytes 9220
  (111 other events, 367.4 us)
Sparse Core Ops, SparseCore 0:
  10.2 68.2 all-gather.5
  80.7 39.6 all-gather.7
  122.6 78.6 all-gather.9
  203.3 78.0 all-gather.11
  493.7 66.6 reduce-scatter.6
  930.2 125.1 reduce-scatter.12
  1059.4 162.4 reduce-scatter.8
  1226.0 162.5 reduce-scatter.10
  1392.5 48.2 all-reduce.22
